TPU v7x, 512 devices: a whole 4x4x16 slice. The times are simulated.
512 devices in a mesh: row: 32 (over z, y_lo), col: 16 (over y_hi, x, core).
Axes of the slice: x: 4, y: 4 (y_hi: 2, y_lo: 2; y = y_hi * 2 + y_lo), z: 16, core: 2. Of those that a mesh axis runs over, the one named last changes fastest.
Arguments:
- coords: int32 [3, 65536], P(None, ('row', 'col')), may hold values from 0 to 60809, as said below
- mode_shapes: bfloat16 [256, 65536], P(None, ('row', 'col')), as said below
- output_shapes: bfloat16 [1048576, 256], P(('row', 'col')), may hold values from -0.375 to 0.375
- response_gain: float32 [2, 256], replicated, may hold values from -4 to 4
Outputs:
- response_power: float32 [1048576], P(('row', 'col'))
- modal_csd: float32 [256, 256], replicated
Inputs may be any that keep to these rules, and one draw needn't show every extreme that they name: `coords`: positions of points on an aircraft's skin, numbered in no spatial order. `mode_shapes`: entries are of order 1 / sqrt(65536); each mode has a share of one sign over all nodes.
All inputs are finite; a program needn't handle non-finite values.
Results may differ from a plain program's by a relative error of at most 0.002.
Values may be sent and summed in bfloat16 or wider, within the bound.
A program may use at most 64 MiB of HBM per device.

v0:
```python
import math
import jax
import jax.numpy as jnp
from jax import lax
from jax.sharding import PartitionSpec as P

wave_scale = 0.35 / 64.0


def coherence(left_points, right_points):
    difference = (left_points[:, :, None] - right_points[:, None, :]).astype(jnp.float32)
    squared = jnp.sum(difference * difference, axis=0)
    return jnp.sinc(wave_scale * jnp.sqrt(squared)).astype(jnp.bfloat16)


def split_parts(matrix):
    high_part = matrix.astype(jnp.bfloat16)
    low_part = (matrix - high_part.astype(jnp.float32)).astype(jnp.bfloat16)
    return (high_part, low_part)


def modal_product(node_shapes, node_projection):
    high_part, low_part = split_parts(node_projection)
    dims = (((1,), (1,)), ((), ()))
    upper = lax.dot_general(node_shapes, high_part, dims, preferred_element_type=jnp.float32)
    lower = lax.dot_general(node_shapes, low_part, dims, preferred_element_type=jnp.float32)
    return upper + lower


def local(coords, mode_shapes, output_shapes, response_gain):
    row_shapes, row_points = (
        lax.all_gather(mode_shapes, "col", axis=1, tiled=True),
        lax.all_gather(coords, "col", axis=1, tiled=True),
    )
    mode_count = mode_shapes.shape[0]
    zero_block = jnp.zeros((mode_count, row_points.shape[1]), jnp.float32)
    piece_shapes = lax.all_gather(mode_shapes, "row", axis=1, tiled=True)
    piece_points = lax.all_gather(coords, "row", axis=1, tiled=True)
    length = piece_shapes.shape[1]
    block_size = math.gcd(length, 1024)
    block_count = length // block_size

    def add_block(loop_index, running_sum):
        block_start = loop_index * block_size
        part_shapes = lax.dynamic_slice_in_dim(piece_shapes, block_start, block_size, 1)
        part_points = lax.dynamic_slice_in_dim(piece_points, block_start, block_size, 1)
        coherence_tile = coherence(part_points, row_points)
        return running_sum + jnp.dot(
            part_shapes, coherence_tile, preferred_element_type=jnp.float32
        )

    projection = lax.fori_loop(0, block_count, add_block, zero_block)
    partial_csd = modal_product(row_shapes, projection)
    modal_csd = lax.psum(partial_csd, ("row", "col"))
    real_part = response_gain[0]
    imag_part = response_gain[1]
    weighted = (
        real_part[:, None] * real_part[None, :] + imag_part[:, None] * imag_part[None, :]
    ) * modal_csd
    weighted_high, weighted_low = split_parts(weighted)
    mapped = jnp.dot(output_shapes, weighted_high, preferred_element_type=jnp.float32)
    mapped = mapped + jnp.dot(output_shapes, weighted_low, preferred_element_type=jnp.float32)
    response_power = jnp.sum(mapped * output_shapes.astype(jnp.float32), axis=1)
    return (response_power, modal_csd)


def solution(mesh):
    in_specs = (P(None, ("row", "col")), P(None, ("row", "col")), P(("row", "col"), None), P())
    out_specs = (P(("row", "col")), P())
    return jax.shard_map(local, mesh=mesh, in_specs=in_specs, out_specs=out_specs, check_vma=False)
```

profile of v0, /device:TPU:4, one launch (start us, length us, event | category | flops | bytes accessed | tf_op | source)
XLA Modules:
  0.0 702.3 jit_solution(17819532380165018910)
XLA Ops:
  7.2 0.0 all-gather.3.cloned.1.call-start
  7.2 0.7 all-gather.3.cloned.1.call-update
  7.9 0.0 all-gather.5.cloned.1.call-start
  7.9 0.7 all-gather.5.cloned.1.call-update
  8.6 0.0 all-reduce.2.cloned.1.call-start
  8.7 69.6 %all_gather.13 = s32[3,4096]{1,0:T(4,128)S(1)} all-gather(s32[3,128]{1,0:T(4,128)} %param.6), channel_id=1, replica_groups=mesh['row'=32,'col'=16] {'row'}, dimensions={1}, use_global_device_ids=true | all-gather | bytes 50688 | tf_op jit(solution)/shard_map/all_gather | solution.py:38
  78.3 19.8 %all_gather.14 = s32[3,2048]{1,0:T(4,128)S(1)} all-gather(s32[3,128]{1,0:T(4,128)} %param.6), channel_id=1, replica_groups=mesh['row'=32,'col'=16] {'col'}, dimensions={1}, use_global_device_ids=true | all-gather | bytes 26112 | tf_op jit(solution)/shard_map/all_gather | solution.py:33
  98.1 2.3 copy.8
  100.4 50.3 %all-gather.3.cloned.1.call-done = bf16[256,4096]{1,0:T(8,128)(2,1)} async-done(((bf16[256,128]{1,0:T(8,128)(2,1)}), bf16[256,4096]{1,0:T(8,128)(2,1)}) %all-gather.3.cloned.1.call-update) | async-done | bytes 2097168 | tf_op jit(solution)/shard_map/all_gather | solution.py:37
  150.7 81.9 %while.16 = (s32[]{:T(128)}, f32[256,2048]{1,0:T(8,128)S(1)}, bf16[256,4096]{1,0:T(8,128)(2,1)}, s32[3,4096]{1,0:T(4,128)S(1)}, s32[3,2048]{1,0:T(4,128)S(1)}, /*index=5*/s32[]{:T(128)}, s32[]{:T(128)}, s32[]{:T(128)}, s32[]{:T(128)}) while((s32[]{:T(128)}, f32[256,2048]{1,0:T(8,128)S(1)}, bf16[256,4096]{1,0:T(8,128)(2,1)}, ...), condition=%wide.region_2.3_spmd.clone, body=%wide.region_0.2_spmd.clone.sunk | while | flops 1171259392 | bytes 21557404 | solution.py:52
  150.7 6.3 multiply_reduce_fusion.2
  157.0 14.1 %fusion.60 = f32[256,2048]{1,0:T(8,128)S(1)} fusion(f32[1024,2048]{1,0:T(8,128)} %multiply_reduce_fusion.2, f32[256,2048]{1,0:T(8,128)S(1)} %get-tuple-element.211, pred[]{:T(512)S(6)} %compare.3, bf16[256,4096]{1,0:T(8,128)(2,1)} %get-tuple-element.221, s32[]{:T(128)S(6)} %select_n.137), kind=kOutput, calls=%fused_computation.26.clone.1 | convolution fusion | flops 1148190720 | bytes 13107205 | tf_op jit(solution)/shard_map/while/body/eval_jaxpr/dot_general | solution.py:48
  171.2 6.3 multiply_reduce_fusion.2
  177.5 14.1 %fusion.60 = f32[256,2048]{1,0:T(8,128)S(1)} fusion(f32[1024,2048]{1,0:T(8,128)} %multiply_reduce_fusion.2, f32[256,2048]{1,0:T(8,128)S(1)} %get-tuple-element.211, pred[]{:T(512)S(6)} %compare.3, bf16[256,4096]{1,0:T(8,128)(2,1)} %get-tuple-element.221, s32[]{:T(128)S(6)} %select_n.137), kind=kOutput, calls=%fused_computation.26.clone.1 | convolution fusion | flops 1148190720 | bytes 13107205 | tf_op jit(solution)/shard_map/while/body/eval_jaxpr/dot_general | solution.py:48
  191.7 6.3 multiply_reduce_fusion.2
  198.0 14.1 %fusion.60 = f32[256,2048]{1,0:T(8,128)S(1)} fusion(f32[1024,2048]{1,0:T(8,128)} %multiply_reduce_fusion.2, f32[256,2048]{1,0:T(8,128)S(1)} %get-tuple-element.211, pred[]{:T(512)S(6)} %compare.3, bf16[256,4096]{1,0:T(8,128)(2,1)} %get-tuple-element.221, s32[]{:T(128)S(6)} %select_n.137), kind=kOutput, calls=%fused_computation.26.clone.1 | convolution fusion | flops 1148190720 | bytes 13107205 | tf_op jit(solution)/shard_map/while/body/eval_jaxpr/dot_general | solution.py:48
  212.1 6.3 multiply_reduce_fusion.2
  218.5 14.1 %fusion.60 = f32[256,2048]{1,0:T(8,128)S(1)} fusion(f32[1024,2048]{1,0:T(8,128)} %multiply_reduce_fusion.2, f32[256,2048]{1,0:T(8,128)S(1)} %get-tuple-element.211, pred[]{:T(512)S(6)} %compare.3, bf16[256,4096]{1,0:T(8,128)(2,1)} %get-tuple-element.221, s32[]{:T(128)S(6)} %select_n.137), kind=kOutput, calls=%fused_computation.26.clone.1 | convolution fusion | flops 1148190720 | bytes 13107205 | tf_op jit(solution)/shard_map/while/body/eval_jaxpr/dot_general | solution.py:48
  232.6 1.8 fusion.37
  234.4 2.4 fusion.35
  236.9 453.2 %all-reduce.2.cloned.1.call-done = f32[256,256]{0,1:T(8,128)} async-done(((f32[256,256]{0,1:T(8,128)}), f32[256,256]{0,1:T(8,128)}) %all-reduce.2.cloned.1.call-update) | async-done | bytes 262160 | tf_op jit(solution)/shard_map/psum | solution.py:54
  690.1 1.8 copy.9
  691.9 1.4 fusion.40
  693.3 2.5 fusion.34
  (12 shorter events, 0.1 us)
Async XLA Ops:
  7.2 143.5 %all-gather.3.cloned.1.call-start = ((), (), s32[]{:S(2)}) async-start(), calls=%async_computation | async-start | bytes 2162688 | tf_op jit(solution)/shard_map/all_gather | solution.py:37
  7.9 224.7 %all-gather.5.cloned.1.call-start = ((), (), s32[]{:S(2)}) async-start(), calls=%async_computation.1 | async-start | bytes 1114112 | tf_op jit(solution)/shard_map/all_gather | solution.py:32
  8.6 681.4 %all-reduce.2.cloned.1.call-start = ((), (), s32[]{:S(2)}) async-start(), calls=%async_computation.2 | async-start | bytes 524288 | tf_op jit(solution)/shard_map/psum | solution.py:54
  150.7 86.2 %copy-start.1 = (f32[2,256]{1,0:T(2,128)S(1)}, f32[2,256]{1,0:T(2,128)}, u32[]{:S(2)}) copy-start(f32[2,256]{1,0:T(2,128)} %param.9) | copy-start | bytes 6148
  232.6 459.3 %copy-start = (bf16[2048,256]{1,0:T(8,128)(2,1)S(1)}, bf16[2048,256]{1,0:T(8,128)(2,1)}, u32[]{:S(2)}) copy-start(bf16[2048,256]{1,0:T(8,128)(2,1)} %param.8) | copy-start | bytes 3145732
Sparse Core Ops, SparseCore 0:
  10.0 140.6 all-gather.2
  153.8 55.1 all-gather.4
  237.0 453.0 all-reduce.1
where the time goes:
time: 703 us; the launch traced here: 702 us
  waiting for transfers between devices  505 us (72%)
  blocking collectives  89.4 us (13%)
  matrix products  64.5 us (9%)
  other arithmetic  25.3 us (4%)
  between operations  13.8 us (2%)
    psum x1, waiting for transfers between devices, local(): modal_csd = lax.psum(partial_csd, ('row', 'col'))  453 us
    all_gather x1, blocking collectives, local(): piece_points = lax.all_gather(coords, 'row', axis=1, tiled=True)  69.6 us
    dot_general x4, matrix products, add_block(): jnp.dot(part_shapes, coherence_tile, preferred_element_type=jnp.float32)  56.4 us
    all_gather x1, waiting for transfers between devices, local(): piece_shapes = lax.all_gather(mode_shapes, 'row', axis=1, tiled=True)  50.3 us
    reduce_sum x4, other arithmetic, coherence(): squared = jnp.sum(difference * difference, axis=0)  25.3 us
    all_gather x1, blocking collectives, local(): lax.all_gather(coords, 'col', axis=1, tiled=True)  19.8 us
  transfers between devices with their start and end apart: 3, of which 2 were waited for; matrix products, arithmetic and copies ran while one was open for 12% of the time, Pallas kernels for 0%

commit v1 on v0

--- a/solution.py
+++ b/solution.py
@@ -51,7 +51,8 @@
 
     projection = lax.fori_loop(0, block_count, add_block, zero_block)
     partial_csd = modal_product(row_shapes, projection)
-    modal_csd = lax.psum(partial_csd, ("row", "col"))
+    one_axis = lax.psum(partial_csd, "row")
+    modal_csd = lax.psum(one_axis, "col")
     real_part = response_gain[0]
     imag_part = response_gain[1]
     weighted = (

time: 703 us -> 661 us (0.940)
  the two profiles are of different devices: /device:TPU:4 before, /device:TPU:1 now
where the time goes in v1:
time: 661 us
  waiting for transfers between devices  460 us (70%)
  blocking collectives  95.3 us (14%)
  matrix products  64.1 us (10%)
  other arithmetic  25.3 us (4%)
  between operations  13.8 us (2%)
    psum x1, waiting for transfers between devices, local(): one_axis = lax.psum(partial_csd, 'row')  258 us
    psum x1, waiting for transfers between devices, local(): modal_csd = lax.psum(one_axis, 'col')  174 us
    all_gather x1, blocking collectives, local(): piece_points = lax.all_gather(coords, 'row', axis=1, tiled=True)  57.3 us
    dot_general x4, matrix products, add_block(): jnp.dot(part_shapes, coherence_tile, preferred_element_type=jnp.float32)  56.4 us
    all_gather x1, blocking collectives, local(): lax.all_gather(coords, 'col', axis=1, tiled=True)  37.9 us
    all_gather x1, waiting for transfers between devices, local(): piece_shapes = lax.all_gather(mode_shapes, 'row', axis=1, tiled=True)  25.8 us
    reduce_sum x4, other arithmetic, coherence(): squared = jnp.sum(difference * difference, axis=0)  25.3 us
  transfers between devices with their start and end apart: 4, of which 3 were waited for; matrix products, arithmetic and copies ran while one was open for 12% of the time, Pallas kernels for 0%

profile of v1, /device:TPU:1, one launch (start us, length us, event | category | flops | bytes accessed | tf_op | source)
XLA Modules:
  0.0 661.0 jit_solution(8721217293561054715)
XLA Ops:
  7.2 0.7 all-gather.3.cloned.1.call-update
  7.9 0.7 all-gather.5.cloned.1.call-update
  8.6 0.0 all-reduce.3.cloned.1.call-start
  8.7 57.3 %all_gather.13 = s32[3,4096]{1,0:T(4,128)S(1)} all-gather(s32[3,128]{1,0:T(4,128)} %param.6), channel_id=1, replica_groups=mesh['row'=32,'col'=16] {'row'}, dimensions={1}, use_global_device_ids=true | all-gather | bytes 50688 | tf_op jit(solution)/shard_map/all_gather | solution.py:38
  66.0 37.9 %all_gather.14 = s32[3,2048]{1,0:T(4,128)S(1)} all-gather(s32[3,128]{1,0:T(4,128)} %param.6), channel_id=1, replica_groups=mesh['row'=32,'col'=16] {'col'}, dimensions={1}, use_global_device_ids=true | all-gather | bytes 26112 | tf_op jit(solution)/shard_map/all_gather | solution.py:33
  104.0 25.8 %all-gather.3.cloned.1.call-done = bf16[256,4096]{1,0:T(8,128)(2,1)} async-done(((bf16[256,128]{1,0:T(8,128)(2,1)}), bf16[256,4096]{1,0:T(8,128)(2,1)}) %all-gather.3.cloned.1.call-update) | async-done | bytes 2097168 | tf_op jit(solution)/shard_map/all_gather | solution.py:37
  129.8 81.9 %while.16 = (s32[]{:T(128)}, f32[256,2048]{1,0:T(8,128)S(1)}, bf16[256,4096]{1,0:T(8,128)(2,1)}, s32[3,4096]{1,0:T(4,128)S(1)}, s32[3,2048]{1,0:T(4,128)S(1)}, /*index=5*/s32[]{:T(128)}, s32[]{:T(128)}, s32[]{:T(128)}, s32[]{:T(128)}) while((s32[]{:T(128)}, f32[256,2048]{1,0:T(8,128)S(1)}, bf16[256,4096]{1,0:T(8,128)(2,1)}, ...), condition=%wide.region_2.3_spmd.clone, body=%wide.region_0.2_spmd.clone.sunk | while | flops 1171259392 | bytes 21557404 | solution.py:52
  129.9 6.3 multiply_reduce_fusion.2
  136.2 14.1 %fusion.60 = f32[256,2048]{1,0:T(8,128)S(1)} fusion(f32[1024,2048]{1,0:T(8,128)} %multiply_reduce_fusion.2, f32[256,2048]{1,0:T(8,128)S(1)} %get-tuple-element.211, pred[]{:T(512)S(6)} %compare.3, bf16[256,4096]{1,0:T(8,128)(2,1)} %get-tuple-element.221, s32[]{:T(128)S(6)} %select_n.137), kind=kOutput, calls=%fused_computation.26.clone.1 | convolution fusion | flops 1148190720 | bytes 13107205 | tf_op jit(solution)/shard_map/while/body/eval_jaxpr/dot_general | solution.py:48
  150.3 6.3 multiply_reduce_fusion.2
  156.7 14.1 %fusion.60 = f32[256,2048]{1,0:T(8,128)S(1)} fusion(f32[1024,2048]{1,0:T(8,128)} %multiply_reduce_fusion.2, f32[256,2048]{1,0:T(8,128)S(1)} %get-tuple-element.211, pred[]{:T(512)S(6)} %compare.3, bf16[256,4096]{1,0:T(8,128)(2,1)} %get-tuple-element.221, s32[]{:T(128)S(6)} %select_n.137), kind=kOutput, calls=%fused_computation.26.clone.1 | convolution fusion | flops 1148190720 | bytes 13107205 | tf_op jit(solution)/shard_map/while/body/eval_jaxpr/dot_general | solution.py:48
  170.8 6.3 multiply_reduce_fusion.2
  177.2 14.1 %fusion.60 = f32[256,2048]{1,0:T(8,128)S(1)} fusion(f32[1024,2048]{1,0:T(8,128)} %multiply_reduce_fusion.2, f32[256,2048]{1,0:T(8,128)S(1)} %get-tuple-element.211, pred[]{:T(512)S(6)} %compare.3, bf16[256,4096]{1,0:T(8,128)(2,1)} %get-tuple-element.221, s32[]{:T(128)S(6)} %select_n.137), kind=kOutput, calls=%fused_computation.26.clone.1 | convolution fusion | flops 1148190720 | bytes 13107205 | tf_op jit(solution)/shard_map/while/body/eval_jaxpr/dot_general | solution.py:48
  191.3 6.3 multiply_reduce_fusion.2
  197.6 14.1 %fusion.60 = f32[256,2048]{1,0:T(8,128)S(1)} fusion(f32[1024,2048]{1,0:T(8,128)} %multiply_reduce_fusion.2, f32[256,2048]{1,0:T(8,128)S(1)} %get-tuple-element.211, pred[]{:T(512)S(6)} %compare.3, bf16[256,4096]{1,0:T(8,128)(2,1)} %get-tuple-element.221, s32[]{:T(128)S(6)} %select_n.137), kind=kOutput, calls=%fused_computation.26.clone.1 | convolution fusion | flops 1148190720 | bytes 13107205 | tf_op jit(solution)/shard_map/while/body/eval_jaxpr/dot_general | solution.py:48
  211.8 1.7 fusion.37
  213.5 2.4 fusion.35
  215.9 0.0 all-reduce.5.cloned.1.call-start
  216.0 258.1 %all-reduce.3.cloned.1.call-done = f32[256,256]{0,1:T(8,128)} async-done(((f32[256,256]{0,1:T(8,128)}), f32[256,256]{0,1:T(8,128)}) %all-reduce.3.cloned.1.call-update) | async-done | bytes 262160 | tf_op jit(solution)/shard_map/psum | solution.py:54
  474.1 0.6 copy.8
  474.8 174.3 %all-reduce.5.cloned.1.call-done = f32[256,256]{0,1:T(8,128)} async-done(((f32[256,256]{0,1:T(8,128)}), f32[256,256]{0,1:T(8,128)}) %all-reduce.5.cloned.1.call-update) | async-done | bytes 262160 | tf_op jit(solution)/shard_map/psum | solution.py:55
  649.1 1.8 copy.9
  650.9 1.4 fusion.40
  652.4 2.1 fusion.34
  (15 shorter events, 0.2 us)
Async XLA Ops:
  7.2 122.7 %all-gather.3.cloned.1.call-start = ((), (), s32[]{:S(2)}) async-start(), calls=%async_computation | async-start | bytes 2162688 | tf_op jit(solution)/shard_map/all_gather | solution.py:37
  7.9 203.9 %all-gather.5.cloned.1.call-start = ((), (), s32[]{:S(2)}) async-start(), calls=%async_computation.1 | async-start | bytes 1114112 | tf_op jit(solution)/shard_map/all_gather | solution.py:32
  8.6 465.5 %all-reduce.3.cloned.1.call-start = ((), (), s32[]{:S(2)}) async-start(), calls=%async_computation.2 | async-start | bytes 524288 | tf_op jit(solution)/shard_map/psum | solution.py:54
  129.8 344.3 %copy-start = (bf16[2048,256]{1,0:T(8,128)(2,1)S(1)}, bf16[2048,256]{1,0:T(8,128)(2,1)}, u32[]{:S(2)}) copy-start(bf16[2048,256]{1,0:T(8,128)(2,1)} %param.8) | copy-start | bytes 3145732
  211.8 263.0 %copy-start.1 = (f32[2,256]{1,0:T(2,128)S(1)}, f32[2,256]{1,0:T(2,128)}, u32[]{:S(2)}) copy-start(f32[2,256]{1,0:T(2,128)} %param.9) | copy-start | bytes 6148
  215.9 433.2 %all-reduce.5.cloned.1.call-start = ((), (), s32[]{:S(2)}) async-start(), calls=%async_computation.3 | async-start | bytes 524288 | tf_op jit(solution)/shard_map/psum | solution.py:55
Sparse Core Ops, SparseCore 0:
  10.0 119.7 all-gather.2
  133.0 78.7 all-gather.4
  216.1 257.9 all-reduce.2
  477.1 171.9 all-reduce.4
